TPU v7x, 1024 devices: a whole 8x8x8 slice. The times are simulated.
1024 devices in a mesh: grid: 64 (over y, x), day: 16 (over z, core).
Axes of the slice: x: 8, y: 8, z: 8, core: 2. Of those that a mesh axis runs over, the one named last changes fastest.
Arguments:
- fields: bfloat16 [6144, 262144], P('day', 'grid')
- eof_basis: bfloat16 [262144, 128], P('grid'), may hold values from -0.01171875 to 0.01171875
- seed_days: int32 [16], replicated, may hold values from 0 to 6143, as said below
Outputs:
- memberships: float32 [6144, 16], P('day')
- regime_centers: float32 [16, 128], replicated
- composites: float32 [16, 262144], P(None, 'grid')
Inputs may be any that keep to these rules, and one draw needn't show every extreme that they name: `seed_days`: 16 distinct days of the record.
All inputs are finite; a program needn't handle non-finite values.
Results may differ from a plain program's by a relative error of at most 0.00043.
Values sent between devices are 32-bit elements; how exact they have to be, the bound alone decides.
No kernel may reach another device: no remote copies, remote signals or barrier semaphores. Data moves between devices by JAX's collectives and lax.ppermute only.
A program may use at most 32 MiB of HBM per device.

v0:
```python
import jax
import jax.numpy as jnp
from jax import lax
from jax.sharding import PartitionSpec as P

ITERS = 3


def member_of(amplitudes, centers):
    offsets = amplitudes[:, None, :] - centers[None, :, :]
    mean_square = jnp.mean(offsets * offsets, axis=2) + 1e-05
    weights = 1.0 / mean_square
    return weights / jnp.sum(weights, axis=1, keepdims=True)


def seed_terms(seed_days, first, amplitudes):
    positions = first + jnp.arange(amplitudes.shape[0], dtype=jnp.int32)
    selector = (seed_days[:, None] == positions[None, :]).astype(jnp.float32)
    return jnp.dot(selector, amplitudes, precision=lax.Precision.HIGHEST)


def regime_terms(amplitudes, centers):
    member = member_of(amplitudes, centers)
    squared = member * member
    numerator = jnp.dot(squared.T, amplitudes, precision=lax.Precision.HIGHEST)
    return (numerator, jnp.sum(squared, axis=0))


def on_device(fields, eof_basis, seed_days):
    day_rows = fields.shape[0]
    partial_value = jnp.dot(fields, eof_basis, preferred_element_type=jnp.float32)
    amplitudes = lax.psum(partial_value, "grid")
    first = lax.axis_index("day") * day_rows
    centers = lax.psum(seed_terms(seed_days, first, amplitudes), "day")
    for sweep in range(ITERS):
        numerator, denominator = lax.psum(regime_terms(amplitudes, centers), "day")
        centers = numerator / denominator[:, None]
    member_all = member_of(amplitudes, centers)
    squares = member_all * member_all
    weights_bf = squares.astype(jnp.bfloat16)
    weighted = jnp.dot(weights_bf.T, fields, preferred_element_type=jnp.float32)
    totals, weight_sums = lax.psum((weighted, jnp.sum(squares, axis=0)), "day")
    return (member_all, centers, totals / weight_sums[:, None])


def solution(mesh):
    placed = (P("day", "grid"), P("grid", None), P())
    return jax.shard_map(
        on_device,
        mesh=mesh,
        in_specs=placed,
        out_specs=(P("day", None), P(), P(None, "grid")),
        check_vma=False,
    )
```

profile of v0, /device:TPU:1, one launch (start us, length us, event | category | flops | bytes accessed | tf_op | source)
XLA Modules:
  0.0 429.4 jit_solution(16621577029129455998)
XLA Ops:
  7.2 1.8 copy-done
  9.1 2.9 fusion.11
  12.0 0.0 all-reduce.8.cloned.1.call-start
  12.0 172.7 %all-reduce.6.cloned.1.call-done = f32[384,128]{1,0:T(8,128)} async-done(((f32[384,128]{1,0:T(8,128)}), f32[384,128]{1,0:T(8,128)}) %all-reduce.6.cloned.1.call-update) | async-done | bytes 196624 | tf_op jit(solution)/shard_map/psum | solution.py:32
  184.7 1.2 fusion.1
  185.9 30.5 %psum.71 = f32[16,128]{1,0:T(8,128)S(1)} all-reduce(f32[16,128]{1,0:T(8,128)S(1)} %fusion.1), channel_id=1, replica_groups=mesh['grid'=64,'day'=16] {'day'}, use_global_device_ids=true, to_apply=%region_1.0 | all-reduce | flops 2048 | bytes 16384 | tf_op jit(solution)/shard_map/psum | solution.py:34
  216.4 1.8 multiply_reduce_fusion.3
  218.2 0.2 divide_reduce_fusion.3
  218.4 0.1 fusion.5
  218.5 1.5 fusion.6
  220.0 23.9 %all-reduce.2 = (f32[16,128]{1,0:T(8,128)S(1)}, f32[16]{0:T(128)S(1)}) all-reduce(f32[16,128]{1,0:T(8,128)S(1)} %fusion.6, f32[16]{0:T(128)S(1)} %fusion.5), channel_id=1, replica_groups=mesh['grid'=64,'day'=16] {'day'}, use_global_device_ids=true, to_apply=%region_4.0 | all-reduce | flops 2064 | bytes 16512 | tf_op jit(solution)/shard_map/psum | solution.py:36
  244.0 0.1 broadcast_divide_fusion.3
  244.0 1.8 multiply_reduce_fusion.2
  245.9 0.2 divide_reduce_fusion.2
  246.0 0.1 fusion.7
  246.2 1.5 fusion.8
  247.6 24.9 %all-reduce.1 = (f32[16,128]{1,0:T(8,128)S(1)}, f32[16]{0:T(128)S(1)}) all-reduce(f32[16,128]{1,0:T(8,128)S(1)} %fusion.8, f32[16]{0:T(128)S(1)} %fusion.7), channel_id=1, replica_groups=mesh['grid'=64,'day'=16] {'day'}, use_global_device_ids=true, to_apply=%region_9.0 | all-reduce | flops 2064 | bytes 16512 | tf_op jit(solution)/shard_map/psum | solution.py:36
  272.5 0.1 broadcast_divide_fusion.2
  272.6 0.9 multiply_reduce_fusion.1
  273.5 0.2 divide_reduce_fusion.1
  273.6 0.1 fusion.9
  273.8 0.5 fusion.10
  274.3 24.5 %all-reduce = (f32[16,128]{1,0:T(8,128)S(1)}, f32[16]{0:T(128)S(1)}) all-reduce(f32[16,128]{1,0:T(8,128)S(1)} %fusion.10, f32[16]{0:T(128)S(1)} %fusion.9), channel_id=1, replica_groups=mesh['grid'=64,'day'=16] {'day'}, use_global_device_ids=true, to_apply=%region_14.0 | all-reduce | flops 2064 | bytes 16512 | tf_op jit(solution)/shard_map/psum | solution.py:36
  298.8 0.1 broadcast_divide_fusion.1
  298.9 0.9 multiply_reduce_fusion
  299.8 0.2 divide_reduce_fusion
  300.0 0.1 multiply_reduce_fusion.4
  300.1 1.3 fusion
  301.4 0.7 copy.6
  302.1 23.6 %psum.79 = f32[16]{0:T(128)S(1)} all-reduce(f32[16]{0:T(128)S(1)} %get-tuple-element.12), channel_id=1, replica_groups=mesh['grid'=64,'day'=16] {'day'}, use_global_device_ids=true, to_apply=%region_21.0 | all-reduce | flops 16 | bytes 128 | tf_op jit(solution)/shard_map/psum | solution.py:42
  325.7 95.1 %all-reduce.8.cloned.1.call-done = f32[16,4096]{1,0:T(8,128)} async-done(((f32[16,4096]{1,0:T(8,128)}), f32[16,4096]{1,0:T(8,128)}) %all-reduce.8.cloned.1.call-update) | async-done | bytes 262160 | tf_op jit(solution)/shard_map/psum | solution.py:42
  420.8 1.7 broadcast_divide_fusion
  (11 shorter events, 0.1 us)
Async XLA Ops:
  7.2 1.9 copy-start
  7.2 177.5 %copy-start.3 = (s32[16]{0:T(128)S(1)}, s32[16]{0:T(128)}, u32[]{:S(2)}) copy-start(s32[16]{0:T(128)} %param.5) | copy-start | bytes 196
  7.2 177.5 %all-reduce.6.cloned.1.call-start = ((), (), s32[]{:S(2)}) async-start(), calls=%async_computation | async-start | bytes 393216 | tf_op jit(solution)/shard_map/psum | solution.py:32
  12.0 408.9 %all-reduce.8.cloned.1.call-start = ((), (), s32[]{:S(2)}) async-start(), calls=%async_computation.1 | async-start | bytes 524288 | tf_op jit(solution)/shard_map/psum | solution.py:42
  184.7 87.9 %copy-start.1 = (f32[384,128]{1,0:T(8,128)S(1)}, f32[384,128]{1,0:T(8,128)}, u32[]{:S(2)}) copy-start(f32[384,128]{1,0:T(8,128)} %all-reduce.6.cloned.1.call-done) | copy-start | bytes 589828
  298.9 123.7 %copy-start.2 = (f32[16,128]{1,0:T(8,128)}, f32[16,128]{1,0:T(8,128)S(1)}, u32[]{:S(2)}) copy-start(f32[16,128]{1,0:T(8,128)S(1)} %broadcast_divide_fusion.1) | copy-start | bytes 24580
Sparse Core Ops, SparseCore 0:
  12.1 172.5 all-reduce.5
  301.5 119.2 all-reduce.7
where the time goes:
time: 430 us; the launch traced here: 429 us
  waiting for transfers between devices  268 us (62%)
  blocking collectives  127 us (30%)
  between operations  14.1 us (3%)
  matrix products  8.83 us (2%)
  other arithmetic  8.59 us (2%)
    psum x1, waiting for transfers between devices, on_device(): amplitudes = lax.psum(partial_value, 'grid')  173 us
    psum x1, waiting for transfers between devices, on_device(): totals, weight_sums = lax.psum((weighted, jnp.sum(squares, axis=0)), 'day')  95.1 us
    psum x3, blocking collectives, on_device(): numerator, denominator = lax.psum(regime_terms(amplitudes, centers), 'day')  73.3 us
    psum x1, blocking collectives, on_device(): centers = lax.psum(seed_terms(seed_days, first, amplitudes), 'day')  30.5 us
    psum x1, blocking collectives, on_device(): totals, weight_sums = lax.psum((weighted, jnp.sum(squares, axis=0)), 'day')  23.6 us
  transfers between devices with their start and end apart: 2, of which 2 were waited for; matrix products, arithmetic and copies ran while one was open for 0% of the time, Pallas kernels for 0%

commit v1 on v0

v1 whole, which is shorter than its diff:
```python
import jax
import jax.numpy as jnp
from jax import lax
from jax.sharding import PartitionSpec as P

ITERS = 3
K = 128
C = 16


def member_of(amplitudes, centers):
    offsets = amplitudes[:, None, :] - centers[None, :, :]
    mean_square = jnp.mean(offsets * offsets, axis=2) + 1e-05
    weights = 1.0 / mean_square
    return weights / jnp.sum(weights, axis=1, keepdims=True)


def gather_all(value, axis, members):
    copies = jnp.broadcast_to(value[None], (members,) + value.shape)
    return lax.all_to_all(copies, axis, 0, 0)


def on_device(fields, eof_basis, seed_days, *, grids, days):
    rows, points = fields.shape
    partial_value = jnp.dot(fields, eof_basis, preferred_element_type=jnp.float32)
    pieces = lax.all_to_all(
        partial_value.reshape(grids, rows // grids, K), "grid", 0, 0
    )
    own = jnp.sum(pieces, axis=0)
    amplitudes = gather_all(own, "grid", grids).reshape(rows, K)

    first = lax.axis_index("day") * rows
    positions = first + jnp.arange(rows, dtype=jnp.int32)
    selector = (seed_days[:, None] == positions[None, :]).astype(jnp.float32)
    seeds = jnp.dot(selector, amplitudes, precision=lax.Precision.HIGHEST)
    centers = jnp.sum(gather_all(seeds, "day", days), axis=0)
    for sweep in range(ITERS):
        member = member_of(amplitudes, centers)
        squared = member * member
        numerator = jnp.dot(squared.T, amplitudes, precision=lax.Precision.HIGHEST)
        denominator = jnp.sum(squared, axis=0)
        terms = jnp.concatenate(
            [numerator, jnp.pad(denominator[None, :], ((0, 7), (0, K - C)))], axis=0
        )
        totals = jnp.sum(gather_all(terms, "day", days), axis=0)
        centers = totals[:C] / totals[C, :C][:, None]
    member_all = member_of(amplitudes, centers)
    squares = member_all * member_all
    weights_bf = squares.astype(jnp.bfloat16)
    weighted = jnp.dot(weights_bf.T, fields, preferred_element_type=jnp.float32)
    width = points // days
    pieces = lax.all_to_all(
        weighted.reshape(C, days, width).transpose(1, 0, 2), "day", 0, 0
    )
    own = jnp.sum(pieces, axis=0).reshape(C * width // K, K)
    weight_sums = jnp.pad(jnp.sum(squares, axis=0)[None, :], ((0, 7), (0, K - C)))
    both = gather_all(jnp.concatenate([own, weight_sums], axis=0), "day", days)
    whole = both[:, : C * width // K].reshape(days, C, width)
    totals = whole.transpose(1, 0, 2).reshape(C, points)
    weight_sums = jnp.sum(both[:, C * width // K, :C], axis=0)
    return (member_all, centers, totals / weight_sums[:, None])


def solution(mesh):
    placed = (P("day", "grid"), P("grid", None), P())

    def body(fields, eof_basis, seed_days):
        return on_device(
            fields,
            eof_basis,
            seed_days,
            grids=mesh.shape["grid"],
            days=mesh.shape["day"],
        )

    return jax.shard_map(
        body,
        mesh=mesh,
        in_specs=placed,
        out_specs=(P("day", None), P(), P(None, "grid")),
        check_vma=False,
    )
```

time: 430 us -> 169 us (0.39)
  waiting for transfers between devices: 268 us -> 24.8 us
  blocking collectives: 127 us -> 110 us
  between operations: 14.1 us -> 0.82 us
  starting transfers between devices: 0.08 us -> 9.57 us
  local copies, waits for them, and re-layouts: 2.56 us -> 8.84 us
    psum x2 -> x0, waiting for transfers between devices: 268 us -> none  [the longest x1 173 us: on_device(): amplitudes = lax.psum(partial_value, 'grid')]
    psum x5 -> x0, blocking collectives: 127 us -> none  [the longest x3 73.3 us: on_device(): numerator, denominator = lax.psum(regime_terms(amplitudes, centers), 'day')]
    all_to_all x0 -> x6, blocking collectives: none -> 110 us  [the longest x4 68.7 us: gather_all(): return lax.all_to_all(copies, axis, 0, 0)]
    all_to_all x0 -> x2, waiting for transfers between devices: none -> 24.8 us  [gather_all(): return lax.all_to_all(copies, axis, 0, 0)]
    all_to_all x0 -> x2, starting transfers between devices: none -> 9.57 us  [gather_all(): return lax.all_to_all(copies, axis, 0, 0)]
where the time goes in v1:
time: 169 us; the launch traced here: 168 us
  blocking collectives  110 us (65%)
  waiting for transfers between devices  24.8 us (15%)
  starting transfers between devices  9.57 us (6%)
  local copies, waits for them, and re-layouts  8.84 us (5%)
  other arithmetic  8.76 us (5%)
  matrix products  5.29 us (3%)
    all_to_all x4, blocking collectives, gather_all(): return lax.all_to_all(copies, axis, 0, 0)  68.7 us
    all_to_all x1, blocking collectives, on_device(): lax.all_to_all(partial_value.reshape(grids, rows // grids, K), 'grid', 0, 0)  26.4 us
    all_to_all x2, waiting for transfers between devices, gather_all(): return lax.all_to_all(copies, axis, 0, 0)  24.8 us
    all_to_all x1, blocking collectives, on_device(): lax.all_to_all(weighted.reshape(C, days, width).transpose(1, 0, 2), 'day'...  14.5 us
    all_to_all x2, starting transfers between devices, gather_all(): return lax.all_to_all(copies, axis, 0, 0)  9.57 us
    reduce_sum x4, other arithmetic, member_of(): mean_square = jnp.mean(offsets * offsets, axis=2) + 1e-05  3.55 us
  transfers between devices with their start and end apart: 2, of which 2 were waited for; matrix products, arithmetic and copies ran while one was open for 0% of the time, Pallas kernels for 0%

profile of v1, /device:TPU:1, one launch (start us, length us, event | category | flops | bytes accessed | tf_op | source)
XLA Modules:
  0.0 167.7 jit_solution(10736587853619331363)
XLA Ops:
  0.6 1.9 %copy-done = bf16[384,4096]{1,0:T(8,128)(2,1)S(1)} copy-done((bf16[384,4096]{1,0:T(8,128)(2,1)S(1)}, bf16[384,4096]{1,0:T(8,128)(2,1)}, u32[]{:S(2)}) %copy-start) | copy-done | bytes 3145752
  2.5 2.9 %fusion.11 = f32[384,128]{1,0:T(8,128)} fusion(bf16[384,4096]{1,0:T(8,128)(2,1)S(1)} %copy-done, bf16[4096,128]{1,0:T(8,128)(2,1)} %param.4), kind=kOutput, calls=%fused_computation.45 | convolution fusion | flops 402653184 | bytes 4390912 | tf_op jit(solution)/shard_map/dot_general | solution.py:25
  5.4 1.0 reshape.46
  6.4 26.4 %all_to_all.40 = f32[64,6,128]{2,1,0:T(8,128)} all-to-all(f32[64,6,128]{2,1,0:T(8,128)S(1)} %reshape.46), channel_id=1, replica_groups=mesh['grid'=64,'day'=16] {'grid'}, dimensions={0} | all-to-all | bytes 393216 | tf_op jit(solution)/shard_map/all_to_all | solution.py:26
  32.8 1.0 reduce_sum.171
  33.8 0.7 broadcast_in_dim.20
  34.6 5.5 %all-to-all-start.1 = ((f32[64,6,128]{2,1,0:T(8,128)}), f32[64,6,128]{2,1,0:T(8,128)}, u32[]{:S(2)}, u32[]{:S(2)}) async-start(f32[64,6,128]{2,1,0:T(8,128)} %broadcast_in_dim.20), calls=%async_computation.1 | async-start | bytes 524288 | tf_op jit(solution)/shard_map/all_to_all | solution.py:20
  40.1 12.4 %all-to-all-done.1 = f32[64,6,128]{2,1,0:T(8,128)} async-done(((f32[64,6,128]{2,1,0:T(8,128)}), f32[64,6,128]{2,1,0:T(8,128)}, u32[]{:S(2)}, u32[]{:S(2)}) %all-to-all-start.1) | async-done | bytes 196640 | tf_op jit(solution)/shard_map/all_to_all | solution.py:20
  52.4 1.0 sub.20
  53.4 0.2 fusion.1
  53.7 29.9 %all_to_all.41 = f32[16,16,128]{2,1,0:T(8,128)S(1)} all-to-all(f32[16,16,128]{2,1,0:T(8,128)S(1)} %broadcast_in_dim.21), channel_id=1, replica_groups=mesh['grid'=64,'day'=16] {'day'}, dimensions={0} | all-to-all | bytes 262144 | tf_op jit(solution)/shard_map/all_to_all | solution.py:20
  83.6 0.9 multiply_reduce_fusion.3
  84.8 0.5 fusion.6
  85.4 12.9 %all_to_all.42 = f32[16,24,128]{2,1,0:T(8,128)S(1)} all-to-all(f32[16,24,128]{2,1,0:T(8,128)S(1)} %broadcast_in_dim.23), channel_id=1, replica_groups=mesh['grid'=64,'day'=16] {'day'}, dimensions={0} | all-to-all | bytes 393216 | tf_op jit(solution)/shard_map/all_to_all | solution.py:20
  98.4 0.9 multiply_reduce_fusion.2
  99.6 0.5 fusion.8
  100.1 13.0 %all_to_all.43 = f32[16,24,128]{2,1,0:T(8,128)S(1)} all-to-all(f32[16,24,128]{2,1,0:T(8,128)S(1)} %broadcast_in_dim.25), channel_id=1, replica_groups=mesh['grid'=64,'day'=16] {'day'}, dimensions={0} | all-to-all | bytes 393216 | tf_op jit(solution)/shard_map/all_to_all | solution.py:20
  113.2 0.9 multiply_reduce_fusion.1
  114.4 0.5 fusion.10
  115.0 13.0 %all_to_all.44 = f32[16,24,128]{2,1,0:T(8,128)S(1)} all-to-all(f32[16,24,128]{2,1,0:T(8,128)S(1)} %broadcast_in_dim.27), channel_id=1, replica_groups=mesh['grid'=64,'day'=16] {'day'}, dimensions={0} | all-to-all | bytes 393216 | tf_op jit(solution)/shard_map/all_to_all | solution.py:20
  128.1 0.9 multiply_reduce_fusion
  129.3 0.5 fusion
  129.8 14.5 %all_to_all.45 = f32[16,16,256]{2,1,0:T(8,128)} all-to-all(f32[16,16,256]{2,1,0:T(8,128)S(1)} %bitcast.29), channel_id=1, replica_groups=mesh['grid'=64,'day'=16] {'day'}, dimensions={0} | all-to-all | bytes 524288 | tf_op jit(solution)/shard_map/all_to_all | solution.py:52
  144.3 1.0 reduce_sum.187
  145.3 0.7 broadcast_in_dim.29
  146.1 4.1 %all-to-all-start.7 = ((f32[16,40,128]{2,1,0:T(8,128)}), f32[16,40,128]{2,1,0:T(8,128)}, u32[]{:S(2)}, u32[]{:S(2)}) async-start(f32[16,40,128]{2,1,0:T(8,128)} %broadcast_in_dim.29), calls=%async_computation.7 | async-start | bytes 655360 | tf_op jit(solution)/shard_map/all_to_all | solution.py:20
  150.2 0.7 copy.11
  150.9 12.4 %all-to-all-done.7 = f32[16,40,128]{2,1,0:T(8,128)} async-done(((f32[16,40,128]{2,1,0:T(8,128)}), f32[16,40,128]{2,1,0:T(8,128)}, u32[]{:S(2)}, u32[]{:S(2)}) %all-to-all-start.7) | async-done | bytes 327712 | tf_op jit(solution)/shard_map/all_to_all | solution.py:20
  163.3 1.7 slice.38
  165.0 1.0 reshape.49
  166.1 0.9 slice_reduce_fusion
  167.0 0.8 broadcast_divide_fusion
  (35 shorter events, 1.7 us)
Async XLA Ops:
  0.6 1.9 %copy-start = (bf16[384,4096]{1,0:T(8,128)(2,1)S(1)}, bf16[384,4096]{1,0:T(8,128)(2,1)}, u32[]{:S(2)}) copy-start(bf16[384,4096]{1,0:T(8,128)(2,1)} %param.3) | copy-start | bytes 9437188
  2.5 50.9 %copy-start.2 = (s32[16]{0:T(128)S(1)}, s32[16]{0:T(128)}, u32[]{:S(2)}) copy-start(s32[16]{0:T(128)} %param.5) | copy-start | bytes 196
  34.6 17.9 %all-to-all-start.1 = ((f32[64,6,128]{2,1,0:T(8,128)}), f32[64,6,128]{2,1,0:T(8,128)}, u32[]{:S(2)}, u32[]{:S(2)}) async-start(f32[64,6,128]{2,1,0:T(8,128)} %broadcast_in_dim.20), calls=%async_computation.1 | async-start | bytes 524288 | tf_op jit(solution)/shard_map/all_to_all | solution.py:20
  128.1 18.0 %copy-start.1 = (f32[16,128]{1,0:T(8,128)}, f32[16,128]{1,0:T(8,128)S(1)}, u32[]{:S(2)}) copy-start(f32[16,128]{1,0:T(8,128)S(1)} %slice_divide_fusion) | copy-start | bytes 24580
  146.1 17.3 %all-to-all-start.7 = ((f32[16,40,128]{2,1,0:T(8,128)}), f32[16,40,128]{2,1,0:T(8,128)}, u32[]{:S(2)}, u32[]{:S(2)}) async-start(f32[16,40,128]{2,1,0:T(8,128)} %broadcast_in_dim.29), calls=%async_computation.7 | async-start | bytes 655360 | tf_op jit(solution)/shard_map/all_to_all | solution.py:20

commit v2 on v0

v2 whole, which is shorter than its diff:
```python
import functools

import jax
import jax.numpy as jnp
from jax import lax
from jax.experimental import pallas as pl
from jax.experimental.pallas import tpu as pltpu
from jax.sharding import Mesh, PartitionSpec as P

ITERS = 3
K = 128
C = 16
STEPS = 4
HIGHEST = lax.Precision.HIGHEST


def call(kernel, out_shape, *args, name, cost=None):
    flops, moved = cost or (1000000, 500000)
    return pl.pallas_call(
        kernel,
        out_shape=out_shape,
        name=name,
        compiler_params=pltpu.CompilerParams(vmem_limit_bytes=8 << 20),
        cost_estimate=pl.CostEstimate(
            flops=flops, bytes_accessed=moved, transcendentals=0
        ),
    )(*args)


def row_of(column):
    lane = lax.broadcasted_iota(jnp.int32, (C, K), 1)
    sub = lax.broadcasted_iota(jnp.int32, (C, K), 0)
    return jnp.sum(jnp.where(lane == sub, column, 0.0), axis=0, keepdims=True)


def column_of(row):
    lane = lax.broadcasted_iota(jnp.int32, (C, K), 1)
    sub = lax.broadcasted_iota(jnp.int32, (C, K), 0)
    return jnp.sum(jnp.where(lane == sub, row, 0.0), axis=1, keepdims=True)


def member_rows(flipped, centers_flipped):
    sums = []
    for c in range(C):
        offset = flipped - centers_flipped[:, c : c + 1]
        sums.append(jnp.sum(offset * offset, axis=0, keepdims=True))
    mean_square = jnp.concatenate(sums, axis=0) / K + 1e-05
    weights = 1.0 / mean_square
    return weights / jnp.sum(weights, axis=0, keepdims=True)


def total_of(ref):
    total = ref[0]
    for i in range(1, ref.shape[0]):
        total = total + ref[i]
    return total


def centers_from(terms_ref):
    total = total_of(terms_ref)
    return total[:C, 0] / column_of(total[C])


def field_copies(fields_ref, chunks_ref, sem_ref):
    step = chunks_ref.shape[2]
    return [
        pltpu.make_async_copy(
            fields_ref.at[:, pl.ds(i * step, step)], chunks_ref.at[i], sem_ref.at[i]
        )
        for i in range(STEPS)
    ]


def project_kernel(fields_ref, basis_ref, out_ref, chunks_ref, basis_chunks_ref, sem_ref, basis_sem_ref):
    step = chunks_ref.shape[2]
    field_loads = field_copies(fields_ref, chunks_ref, sem_ref)
    basis_loads = [
        pltpu.make_async_copy(
            basis_ref.at[pl.ds(i * step, step)],
            basis_chunks_ref.at[i],
            basis_sem_ref.at[i],
        )
        for i in range(STEPS)
    ]
    for i in range(STEPS):
        basis_loads[i].start()
        field_loads[i].start()
    total = None
    for i in range(STEPS):
        basis_loads[i].wait()
        field_loads[i].wait()
        part = jnp.dot(
            chunks_ref[i], basis_chunks_ref[i], preferred_element_type=jnp.float32
        )
        total = part if total is None else total + part
    grids, own = out_ref.shape[:2]
    for r in range(own):
        out_ref[:, r, 0, :] = total[r * grids : (r + 1) * grids]


def project(fields, basis, grids):
    rows, points = fields.shape
    step = points // STEPS
    return pl.pallas_call(
        project_kernel,
        in_specs=[pl.BlockSpec(memory_space=pltpu.HBM)] * 2,
        out_shape=jax.ShapeDtypeStruct((grids, rows // grids, 1, K), jnp.float32),
        scratch_shapes=[
            pltpu.VMEM((STEPS, rows, step), jnp.bfloat16),
            pltpu.VMEM((STEPS, step, K), jnp.bfloat16),
            pltpu.SemaphoreType.DMA((STEPS,)),
            pltpu.SemaphoreType.DMA((STEPS,)),
        ],
        name="project",
        compiler_params=pltpu.CompilerParams(vmem_limit_bytes=63 << 20),
    )(fields, basis)


def own_rows_kernel(pieces_ref, out_ref):
    total = total_of(pieces_ref)
    out_ref[...] = jnp.broadcast_to(total[None], out_ref.shape)


def seeds_kernel(pieces_ref, wanted_ref, flipped_ref, seeds_ref):
    own = pieces_ref.shape[1]
    amplitudes = jnp.concatenate([pieces_ref[:, r, 0, :] for r in range(own)], axis=0)
    rows = amplitudes.shape[0]
    position = lax.broadcasted_iota(jnp.int32, (C, rows), 1)
    selector = (wanted_ref[...] == position).astype(jnp.float32)
    seeds = jnp.dot(
        selector, amplitudes, precision=HIGHEST, preferred_element_type=jnp.float32
    )
    flipped_ref[...] = amplitudes.T
    seeds_ref[...] = jnp.broadcast_to(seeds[None], seeds_ref.shape)


def store_terms(flipped, centers, out_ref):
    member = member_rows(flipped, centers.T)
    squared = member * member
    numerator = lax.dot_general(
        squared,
        flipped,
        (((1,), (1,)), ((), ())),
        precision=HIGHEST,
        preferred_element_type=jnp.float32,
    )
    weight_row = row_of(jnp.sum(squared, axis=1, keepdims=True))
    for i in range(out_ref.shape[0]):
        out_ref[i, :C, 0, :] = numerator
        out_ref[i, C, :, :] = weight_row


def first_kernel(core_ref, seeds_ref, flipped_ref, other_ref, out_ref, chip_ref):
    rows = flipped_ref.shape[1]

    @pl.when(core_ref[0] == 0)
    def _():
        chip_ref[:, :rows] = flipped_ref[...]
        chip_ref[:, rows:] = other_ref[...]

    @pl.when(core_ref[0] != 0)
    def _():
        chip_ref[:, :rows] = other_ref[...]
        chip_ref[:, rows:] = flipped_ref[...]

    store_terms(chip_ref[...], total_of(seeds_ref), out_ref)


def first_terms(core, seeds, flipped, other, layers):
    rows = flipped.shape[1]
    return pl.pallas_call(
        first_kernel,
        in_specs=[pl.BlockSpec(memory_space=pltpu.SMEM)]
        + [pl.BlockSpec(memory_space=pltpu.VMEM)] * 3,
        out_shape=[
            jax.ShapeDtypeStruct((layers, C + 1, 1, K), jnp.float32),
            jax.ShapeDtypeStruct((K, 2 * rows), jnp.float32),
        ],
        name="first",
        compiler_params=pltpu.CompilerParams(vmem_limit_bytes=8 << 20),
    )(core, seeds, flipped, other)


def sweep_kernel(terms_ref, flipped_ref, out_ref):
    store_terms(flipped_ref[...], centers_from(terms_ref), out_ref)


def weigh_kernel(
    terms_ref,
    flipped_ref,
    fields_ref,
    member_ref,
    centers_ref,
    row_ref,
    out_ref,
    chunks_ref,
    sem_ref,
):
    loads = field_copies(fields_ref, chunks_ref, sem_ref)
    for load in loads:
        load.start()
    centers = centers_from(terms_ref)
    centers_ref[...] = centers
    member = member_rows(flipped_ref[...], centers.T)
    member_ref[...] = member
    squares = member * member
    row_ref[...] = row_of(jnp.sum(squares, axis=1, keepdims=True))
    weights_bf = squares.astype(jnp.bfloat16)
    width = out_ref.shape[2]
    each = out_ref.shape[0] // STEPS
    for i in range(STEPS):
        loads[i].wait()
        part = jnp.dot(weights_bf, chunks_ref[i], preferred_element_type=jnp.float32)
        for j in range(each):
            out_ref[i * each + j] = part[:, j * width : (j + 1) * width]


def weigh(terms, flipped, fields, days):
    rows, points = fields.shape
    vmem = pl.BlockSpec(memory_space=pltpu.VMEM)
    return pl.pallas_call(
        weigh_kernel,
        in_specs=[vmem, vmem, pl.BlockSpec(memory_space=pltpu.HBM)],
        out_shape=[
            jax.ShapeDtypeStruct((C, rows), jnp.float32),
            jax.ShapeDtypeStruct((C, K), jnp.float32),
            jax.ShapeDtypeStruct((1, K), jnp.float32),
            jax.ShapeDtypeStruct((days, C, points // days), jnp.float32),
        ],
        scratch_shapes=[
            pltpu.VMEM((STEPS, rows, points // STEPS), jnp.bfloat16),
            pltpu.SemaphoreType.DMA((STEPS,)),
        ],
        name="weigh",
        compiler_params=pltpu.CompilerParams(vmem_limit_bytes=62 << 20),
    )(terms, flipped, fields)


def own_points_kernel(pieces_ref, row_ref, out_ref):
    total = total_of(pieces_ref)
    tiles = total.shape[1] // K
    for i in range(out_ref.shape[0]):
        for t in range(tiles):
            out_ref[i, t * C : (t + 1) * C, 0, :] = total[:, t * K : (t + 1) * K]
        out_ref[i, tiles * C, :, :] = row_ref[...]


def finish_kernel(pieces_ref, out_ref):
    days, last = pieces_ref.shape[0], pieces_ref.shape[1] - 1
    weight_row = pieces_ref[0, last]
    for j in range(1, days):
        weight_row = weight_row + pieces_ref[j, last]
    weight = column_of(weight_row)
    tiles = last // C
    for j in range(days):
        for t in range(tiles):
            at = (j * tiles + t) * K
            out_ref[:, at : at + K] = pieces_ref[j, t * C : (t + 1) * C, 0, :] / weight


def on_device(fields, eof_basis, seed_days, *, grids, layers):
    rows, points = fields.shape
    days = 2 * layers
    f32 = jnp.float32
    own = rows // grids
    both = ("z", "c")

    def exchange(value, axis):
        return lax.all_to_all(value, axis, 0, 0)

    pieces = exchange(project(fields, eof_basis, grids), "grid")
    shape = jax.ShapeDtypeStruct((grids, own, 1, K), f32)
    pieces = exchange(call(own_rows_kernel, shape, pieces, name="own_rows"), "grid")

    core = lax.axis_index("c")
    first = (2 * lax.axis_index("z") + core) * rows
    flipped, seeds = call(
        seeds_kernel,
        [
            jax.ShapeDtypeStruct((K, rows), f32),
            jax.ShapeDtypeStruct((days, C, K), f32),
        ],
        pieces,
        (seed_days - first)[:, None],
        name="seeds",
    )
    other = lax.ppermute(flipped, "c", [(0, 1), (1, 0)])
    seeds = exchange(seeds, both)
    terms, chip = first_terms(core[None], seeds, flipped, other, layers)
    terms = exchange(terms, "z")
    shape = jax.ShapeDtypeStruct((layers, C + 1, 1, K), f32)
    for sweep in range(1, ITERS):
        terms = exchange(call(sweep_kernel, shape, terms, chip, name="sweep"), "z")

    member, centers, weight_row, weighted = weigh(terms, flipped, fields, days)
    pieces = exchange(weighted, both)
    tiles = points // days // K
    shape = jax.ShapeDtypeStruct((days, tiles * C + 1, 1, K), f32)
    pieces = call(own_points_kernel, shape, pieces, weight_row, name="own_points")
    pieces = exchange(pieces, both)
    shape = jax.ShapeDtypeStruct((C, points), f32)
    composites = call(finish_kernel, shape, pieces, name="finish")
    return (member.T, centers, composites)


def solution(mesh):
    grids, days = mesh.shape["grid"], mesh.shape["day"]
    finer = Mesh(mesh.devices.reshape(grids, days // 2, 2), ("grid", "z", "c"))
    both = ("z", "c")
    return jax.shard_map(
        functools.partial(on_device, grids=grids, layers=days // 2),
        mesh=finer,
        in_specs=(P(both, "grid"), P("grid", None), P()),
        out_specs=(P(both, None), P(), P(None, "grid")),
        check_vma=False,
    )
```

time: 430 us -> 152 us (0.35)
  waiting for transfers between devices: 268 us -> 18.8 us
  blocking collectives: 127 us -> 89 us
  starting transfers between devices: 0.08 us -> 27.2 us
  Pallas kernels: 0 us -> 15.2 us
  between operations: 14.1 us -> 0.73 us
  matrix products: 8.83 us -> 0 us
  other arithmetic: 8.59 us -> 0.01 us
    psum x2 -> x0, waiting for transfers between devices: 268 us -> none  [the longest x1 173 us: on_device(): amplitudes = lax.psum(partial_value, 'grid')]
    psum x5 -> x0, blocking collectives: 127 us -> none  [the longest x3 73.3 us: on_device(): numerator, denominator = lax.psum(regime_terms(amplitudes, centers), 'day')]
    all_to_all x0 -> x6, blocking collectives: none -> 89 us  [exchange(): return lax.all_to_all(value, axis, 0, 0)]
    all_to_all x0 -> x2, starting transfers between devices: none -> 25.2 us  [exchange(): return lax.all_to_all(value, axis, 0, 0)]
    all_to_all x0 -> x2, waiting for transfers between devices: none -> 17.5 us  [exchange(): return lax.all_to_all(value, axis, 0, 0)]
    pallas_call x0 -> x9, Pallas kernels: none -> 15.2 us  [the longest x6 5.78 us: call(): pl.pallas_call(kernel, out_shape=out_shape, name=name, compiler_params=pl...]
    dot_general x6 -> x0, matrix products: 8.83 us -> none  [the longest x3 3.48 us: regime_terms(): numerator = jnp.dot(squared.T, amplitudes, precision=lax.Precision.HIGHEST)]
    reduce_sum x12 -> x0, other arithmetic: 6.62 us -> none  [the longest x4 5.43 us: member_of(): mean_square = jnp.mean(offsets * offsets, axis=2) + 1e-05]
  transfers between devices with their start and end apart: 2 -> 3, of which waited for: 2 -> 3; matrix products, arithmetic and copies ran while one was open for 0% -> 0% of each run, Pallas kernels for 0% -> 0%
where the time goes in v2:
time: 152 us
  blocking collectives  89 us (59%)
  starting transfers between devices  27.2 us (18%)
  waiting for transfers between devices  18.8 us (12%)
  Pallas kernels  15.2 us (10%)
    all_to_all x6, blocking collectives, exchange(): return lax.all_to_all(value, axis, 0, 0)  89 us
    all_to_all x2, starting transfers between devices, exchange(): return lax.all_to_all(value, axis, 0, 0)  25.2 us
    all_to_all x2, waiting for transfers between devices, exchange(): return lax.all_to_all(value, axis, 0, 0)  17.5 us
    pallas_call x6, Pallas kernels, call(): pl.pallas_call(kernel, out_shape=out_shape, name=name, compiler_params=pl...  5.78 us
    pallas_call x1, Pallas kernels, project(): pl.pallas_call(project_kernel, in_specs=[pl.BlockSpec(memory_space=pltpu....  4.26 us
    pallas_call x1, Pallas kernels, weigh(): pl.pallas_call(weigh_kernel, in_specs=[vmem, vmem, pl.BlockSpec(memory_sp...  3.8 us
  transfers between devices with their start and end apart: 3, of which 3 were waited for; matrix products, arithmetic and copies ran while one was open for 0% of the time, Pallas kernels for 0%

profile of v2, /device:TPU:1, one launch (start us, length us, event | category | flops | bytes accessed | tf_op | source)
XLA Modules:
  0.0 151.7 jit_solution(3231941675574187650)
XLA Ops:
  0.6 0.0 copy-start.2
  0.6 4.3 %project.1 = f32[64,6,1,128]{3,2,1,0:T(1,128)} custom-call(bf16[384,4096]{1,0:T(8,128)(2,1)} %fields_ref.3, bf16[4096,128]{1,0:T(8,128)(2,1)} %basis_ref.1), custom_call_target="tpu_custom_call" | custom-call | tf_op jit(solution)/shard_map/project/pallas_call | solution.py:104
  4.9 26.1 %all_to_all.40.pieces_ref = f32[64,6,1,128]{3,2,1,0:T(1,128)S(1)} all-to-all(f32[64,6,1,128]{3,2,1,0:T(1,128)} %project.1), channel_id=1, replica_groups=mesh['grid'=64,'z'=8,'c'=2] {'grid'}, dimensions={0} | all-to-all | bytes 393216 | tf_op jit(solution)/shard_map/all_to_all | solution.py:269
  31.0 0.9 own_rows.1
  31.8 4.6 %all-to-all-start.1 = ((f32[64,6,1,128]{3,2,1,0:T(1,128)}), f32[64,6,1,128]{3,2,1,0:T(1,128)S(1)}, u32[]{:S(2)}, u32[]{:S(2)}) async-start(f32[64,6,1,128]{3,2,1,0:T(1,128)} %own_rows.1), calls=%async_computation.1 | async-start | bytes 393216 | tf_op jit(solution)/shard_map/all_to_all | solution.py:269
  36.5 0.0 copy-done.2
  36.5 0.1 copy.6.wanted_ref
  36.6 11.9 %all-to-all-done.1.pieces_ref = f32[64,6,1,128]{3,2,1,0:T(1,128)S(1)} async-done(((f32[64,6,1,128]{3,2,1,0:T(1,128)}), f32[64,6,1,128]{3,2,1,0:T(1,128)S(1)}, u32[]{:S(2)}, u32[]{:S(2)}) %all-to-all-start.1) | async-done | bytes 196640 | tf_op jit(solution)/shard_map/all_to_all | solution.py:269
  48.5 1.0 seeds.1
  49.4 0.0 copy-start
  49.4 20.6 %all-to-all-start.2 = ((f32[16,16,128]{2,1,0:T(8,128)}), f32[16,16,128]{2,1,0:T(8,128)S(1)}, u32[]{:S(2)}, u32[]{:S(2)}) async-start(f32[16,16,128]{2,1,0:T(8,128)} %get-tuple-element.11), calls=%async_computation.2 | async-start | bytes 262144 | tf_op jit(solution)/shard_map/all_to_all | solution.py:269
  70.1 2.0 %collective-permute-start = (f32[128,384]{1,0:T(8,128)S(1)}, f32[128,384]{1,0:T(8,128)S(1)}, u32[]{:S(2)}, u32[]{:S(2)}) collective-permute-start(f32[128,384]{1,0:T(8,128)S(1)} %get-tuple-element.12.flipped_ref), channel_id=1, source_target_pairs={{0,1},{1,0},{2,3},{3,2},{4,5},{5,4},{6,7},{7,6},{8,9},{9,8},{10,11... | collective-permute-start | bytes 589832 | tf_op jit(solution)/shard_map/ppermute | solution.py:287
  72.1 1.3 collective-permute-done.other_ref
  73.4 5.6 %all-to-all-done.2.seeds_ref = f32[16,16,128]{2,1,0:T(8,128)S(1)} async-done(((f32[16,16,128]{2,1,0:T(8,128)}), f32[16,16,128]{2,1,0:T(8,128)S(1)}, u32[]{:S(2)}, u32[]{:S(2)}) %all-to-all-start.2) | async-done | bytes 131104 | tf_op jit(solution)/shard_map/all_to_all | solution.py:269
  78.9 1.4 first.1
  80.4 9.6 %all_to_all.41.terms_ref = f32[8,17,1,128]{3,2,1,0:T(1,128)S(1)} all-to-all(f32[8,17,1,128]{3,2,1,0:T(1,128)S(1)} %get-tuple-element.13), channel_id=1, replica_groups=mesh['grid'=64,'z'=8,'c'=2] {'z'}, dimensions={0} | all-to-all | bytes 139264 | tf_op jit(solution)/shard_map/all_to_all | solution.py:269
  89.9 1.5 sweep.2
  91.4 9.6 %all_to_all.42.terms_ref = f32[8,17,1,128]{3,2,1,0:T(1,128)S(1)} all-to-all(f32[8,17,1,128]{3,2,1,0:T(1,128)S(1)} %sweep.2), channel_id=1, replica_groups=mesh['grid'=64,'z'=8,'c'=2] {'z'}, dimensions={0} | all-to-all | bytes 139264 | tf_op jit(solution)/shard_map/all_to_all | solution.py:269
  101.0 1.5 sweep.3
  102.5 10.4 %all_to_all.43.terms_ref = f32[8,17,1,128]{3,2,1,0:T(1,128)} all-to-all(f32[8,17,1,128]{3,2,1,0:T(1,128)S(1)} %sweep.3), channel_id=1, replica_groups=mesh['grid'=64,'z'=8,'c'=2] {'z'}, dimensions={0} | all-to-all | bytes 139264 | tf_op jit(solution)/shard_map/all_to_all | solution.py:269
  112.9 0.0 copy-done
  112.9 3.8 %weigh.1 = (f32[16,384]{1,0:T(8,128)}, f32[16,128]{1,0:T(8,128)}, f32[1,128]{1,0:T(1,128)}, f32[16,16,256]{2,1,0:T(8,128)}) custom-call(f32[8,17,1,128]{3,2,1,0:T(1,128)} %all_to_all.43.terms_ref, f32[128,384]{1,0:T(8,128)} %copy-done, bf16[384,4096]{1,0:T(8,128)(2,1)} %fields_ref.3), custom_call_target="tpu_custom_call" | custom-call | tf_op jit(solution)/shard_map/weigh/pallas_call | solution.py:221
  116.7 18.9 %all_to_all.44.pieces_ref = f32[16,16,256]{2,1,0:T(8,128)S(1)} all-to-all(f32[16,16,256]{2,1,0:T(8,128)} %get-tuple-element.17), channel_id=1, replica_groups=mesh['grid'=64,'z'=8,'c'=2] {'z','c'}, dimensions={0} | all-to-all | bytes 524288 | tf_op jit(solution)/shard_map/all_to_all | solution.py:269
  135.6 0.0 copy-start.1
  135.6 0.7 copy-done.1
  136.3 0.2 own_points.1
  136.4 14.4 %all_to_all.45.pieces_ref = f32[16,33,1,128]{3,2,1,0:T(1,128)S(1)} all-to-all(f32[16,33,1,128]{3,2,1,0:T(1,128)S(1)} %own_points.1), channel_id=1, replica_groups=mesh['grid'=64,'z'=8,'c'=2] {'z','c'}, dimensions={0} | all-to-all | bytes 540672 | tf_op jit(solution)/shard_map/all_to_all | solution.py:269
  150.9 0.9 finish.1
  (1 shorter events, 0.0 us)
Async XLA Ops:
  0.6 35.8 %copy-start.2 = (s32[16]{0:T(128)S(1)}, s32[16]{0:T(128)}, u32[]{:S(2)}) copy-start(s32[16]{0:T(128)} %param.5) | copy-start | bytes 196
  31.8 16.6 %all-to-all-start.1 = ((f32[64,6,1,128]{3,2,1,0:T(1,128)}), f32[64,6,1,128]{3,2,1,0:T(1,128)S(1)}, u32[]{:S(2)}, u32[]{:S(2)}) async-start(f32[64,6,1,128]{3,2,1,0:T(1,128)} %own_rows.1), calls=%async_computation.1 | async-start | bytes 393216 | tf_op jit(solution)/shard_map/all_to_all | solution.py:269
  49.4 63.5 %copy-start = (f32[128,384]{1,0:T(8,128)}, f32[128,384]{1,0:T(8,128)S(1)}, u32[]{:S(2)}) copy-start(f32[128,384]{1,0:T(8,128)S(1)} %get-tuple-element.12.flipped_ref) | copy-start | bytes 589828
  49.4 29.5 %all-to-all-start.2 = ((f32[16,16,128]{2,1,0:T(8,128)}), f32[16,16,128]{2,1,0:T(8,128)S(1)}, u32[]{:S(2)}, u32[]{:S(2)}) async-start(f32[16,16,128]{2,1,0:T(8,128)} %get-tuple-element.11), calls=%async_computation.2 | async-start | bytes 262144 | tf_op jit(solution)/shard_map/all_to_all | solution.py:269
  70.1 3.3 %collective-permute-start = (f32[128,384]{1,0:T(8,128)S(1)}, f32[128,384]{1,0:T(8,128)S(1)}, u32[]{:S(2)}, u32[]{:S(2)}) collective-permute-start(f32[128,384]{1,0:T(8,128)S(1)} %get-tuple-element.12.flipped_ref), channel_id=1, source_target_pairs={{0,1},{1,0},{2,3},{3,2},{4,5},{5,4},{6,7},{7,6},{8,9},{9,8},{10,11... | collective-permute-start | bytes 589832 | tf_op jit(solution)/shard_map/ppermute | solution.py:287
  135.6 0.7 copy-start.1

commit v3 on v2

v3 whole, which is shorter than its diff:
```python
import functools

import jax
import jax.numpy as jnp
from jax import lax
from jax.experimental import pallas as pl
from jax.experimental.pallas import tpu as pltpu
from jax.sharding import PartitionSpec as P

ITERS = 3
K = 128
C = 16
BLOCKS = 3
PARTS = 4
HIGHEST = lax.Precision.HIGHEST


def call(kernel, out_shape, *args, name, cost=None):
    flops, moved = cost or (1000000, 500000)
    return pl.pallas_call(
        kernel,
        out_shape=out_shape,
        name=name,
        compiler_params=pltpu.CompilerParams(vmem_limit_bytes=8 << 20),
        cost_estimate=pl.CostEstimate(
            flops=flops, bytes_accessed=moved, transcendentals=0
        ),
    )(*args)


def row_of(column):
    lane = lax.broadcasted_iota(jnp.int32, (C, K), 1)
    sub = lax.broadcasted_iota(jnp.int32, (C, K), 0)
    return jnp.sum(jnp.where(lane == sub, column, 0.0), axis=0, keepdims=True)


def column_of(row):
    lane = lax.broadcasted_iota(jnp.int32, (C, K), 1)
    sub = lax.broadcasted_iota(jnp.int32, (C, K), 0)
    return jnp.sum(jnp.where(lane == sub, row, 0.0), axis=1, keepdims=True)


def member_rows(flipped, centers_flipped):
    sums = []
    for c in range(C):
        offset = flipped - centers_flipped[:, c : c + 1]
        sums.append(jnp.sum(offset * offset, axis=0, keepdims=True))
    mean_square = jnp.concatenate(sums, axis=0) / K + 1e-05
    weights = 1.0 / mean_square
    return weights / jnp.sum(weights, axis=0, keepdims=True)


def total_of(ref):
    total = ref[0]
    for i in range(1, ref.shape[0]):
        total = total + ref[i]
    return total


def centers_from(terms_ref):
    total = total_of(terms_ref)
    return total[:C, 0] / column_of(total[C])


def project_kernel(
    fields_ref, basis_ref, out_ref, chunks_ref, basis_chunks_ref, sem_ref, basis_sem_ref
):
    blocks, rows = chunks_ref.shape[:2]
    parts, step = basis_chunks_ref.shape[:2]
    basis_loads = [
        pltpu.make_async_copy(
            basis_ref.at[pl.ds(j * step, step)],
            basis_chunks_ref.at[j],
            basis_sem_ref.at[j],
        )
        for j in range(parts)
    ]
    loads = [
        pltpu.make_async_copy(
            fields_ref.at[pl.ds(i * rows, rows)], chunks_ref.at[i], sem_ref.at[i]
        )
        for i in range(blocks)
    ]
    for load in basis_loads + loads:
        load.start()
    for load in basis_loads:
        load.wait()
    grids = out_ref.shape[0]
    for i in range(blocks):
        loads[i].wait()
        total = None
        for j in range(parts):
            part = jnp.dot(
                chunks_ref[i, :, j * step : (j + 1) * step],
                basis_chunks_ref[j],
                preferred_element_type=jnp.float32,
            )
            total = part if total is None else total + part
        each = rows // grids
        for r in range(each):
            out_ref[:, i * each + r, 0, :] = total[r * grids : (r + 1) * grids]


def project(fields, basis, grids):
    rows, points = fields.shape
    return pl.pallas_call(
        project_kernel,
        in_specs=[pl.BlockSpec(memory_space=pltpu.HBM)] * 2,
        out_shape=jax.ShapeDtypeStruct((grids, rows // grids, 1, K), jnp.float32),
        scratch_shapes=[
            pltpu.VMEM((BLOCKS, rows // BLOCKS, points), jnp.bfloat16),
            pltpu.VMEM((PARTS, points // PARTS, K), jnp.bfloat16),
            pltpu.SemaphoreType.DMA((BLOCKS,)),
            pltpu.SemaphoreType.DMA((PARTS,)),
        ],
        name="project",
        compiler_params=pltpu.CompilerParams(vmem_limit_bytes=63 << 20),
    )(fields, basis)


def own_rows_kernel(pieces_ref, out_ref):
    total = total_of(pieces_ref)
    out_ref[...] = jnp.broadcast_to(total[None], out_ref.shape)


def seeds_kernel(days_ref, pieces_ref, flipped_ref, seeds_ref):
    own = pieces_ref.shape[1]
    amplitudes = jnp.concatenate([pieces_ref[:, r, 0, :] for r in range(own)], axis=0)
    rows = amplitudes.shape[0]
    first = lax.axis_index("day") * rows
    position = first + lax.broadcasted_iota(jnp.int32, (1, rows), 1)
    selector = jnp.concatenate(
        [(position == days_ref[c]).astype(jnp.float32) for c in range(C)], axis=0
    )
    seeds = jnp.dot(
        selector, amplitudes, precision=HIGHEST, preferred_element_type=jnp.float32
    )
    flipped_ref[...] = amplitudes.T
    seeds_ref[...] = jnp.broadcast_to(seeds[None], seeds_ref.shape)


def store_terms(flipped, centers, out_ref):
    member = member_rows(flipped, centers.T)
    squared = member * member
    numerator = lax.dot_general(
        squared,
        flipped,
        (((1,), (1,)), ((), ())),
        precision=HIGHEST,
        preferred_element_type=jnp.float32,
    )
    weight_row = row_of(jnp.sum(squared, axis=1, keepdims=True))
    for i in range(out_ref.shape[0]):
        out_ref[i, :C, 0, :] = numerator
        out_ref[i, C, :, :] = weight_row


def first_kernel(seeds_ref, flipped_ref, out_ref):
    store_terms(flipped_ref[...], total_of(seeds_ref), out_ref)


def sweep_kernel(terms_ref, flipped_ref, out_ref):
    store_terms(flipped_ref[...], centers_from(terms_ref), out_ref)


def weigh_kernel(
    terms_ref, flipped_ref, fields_ref, member_ref, centers_ref, row_ref, out_ref
):
    centers = centers_from(terms_ref)
    centers_ref[...] = centers
    member = member_rows(flipped_ref[...], centers.T)
    member_ref[...] = member
    squares = member * member
    row_ref[...] = row_of(jnp.sum(squares, axis=1, keepdims=True))
    weights_bf = squares.astype(jnp.bfloat16)
    days, _, width = out_ref.shape
    for j in range(days):
        out_ref[j] = jnp.dot(
            weights_bf,
            fields_ref[:, j * width : (j + 1) * width],
            preferred_element_type=jnp.float32,
        )


def own_points_kernel(pieces_ref, row_ref, out_ref):
    total = total_of(pieces_ref)
    tiles = total.shape[1] // K
    for i in range(out_ref.shape[0]):
        for t in range(tiles):
            out_ref[i, t * C : (t + 1) * C, 0, :] = total[:, t * K : (t + 1) * K]
        out_ref[i, tiles * C, :, :] = row_ref[...]


def finish_kernel(pieces_ref, out_ref):
    days, last = pieces_ref.shape[0], pieces_ref.shape[1] - 1
    weight_row = pieces_ref[0, last]
    for j in range(1, days):
        weight_row = weight_row + pieces_ref[j, last]
    weight = column_of(weight_row)
    tiles = last // C
    for j in range(days):
        for t in range(tiles):
            at = (j * tiles + t) * K
            out_ref[:, at : at + K] = pieces_ref[j, t * C : (t + 1) * C, 0, :] / weight


def on_device(fields, eof_basis, seed_days, *, grids, days):
    rows, points = fields.shape
    f32 = jnp.float32
    own = rows // grids

    def exchange(value, axis):
        return lax.all_to_all(value, axis, 0, 0)

    pieces = exchange(project(fields, eof_basis, grids), "grid")
    shape = jax.ShapeDtypeStruct((grids, own, 1, K), f32)
    pieces = exchange(call(own_rows_kernel, shape, pieces, name="own_rows"), "grid")

    smem = pl.BlockSpec(memory_space=pltpu.SMEM)
    flipped, seeds = pl.pallas_call(
        seeds_kernel,
        in_specs=[smem, pl.BlockSpec(memory_space=pltpu.VMEM)],
        out_shape=[
            jax.ShapeDtypeStruct((K, rows), f32),
            jax.ShapeDtypeStruct((days, C, K), f32),
        ],
        name="seeds",
        compiler_params=pltpu.CompilerParams(vmem_limit_bytes=8 << 20),
    )(seed_days, pieces)
    seeds = exchange(seeds, "day")
    shape = jax.ShapeDtypeStruct((days, C + 1, 1, K), f32)
    terms = exchange(call(first_kernel, shape, seeds, flipped, name="first"), "day")
    for sweep in range(1, ITERS):
        terms = call(sweep_kernel, shape, terms, flipped, name="sweep")
        terms = exchange(terms, "day")

    shapes = [
        jax.ShapeDtypeStruct((C, rows), f32),
        jax.ShapeDtypeStruct((C, K), f32),
        jax.ShapeDtypeStruct((1, K), f32),
        jax.ShapeDtypeStruct((days, C, points // days), f32),
    ]
    member, centers, weight_row, weighted = call(
        weigh_kernel, shapes, terms, flipped, fields, name="weigh"
    )
    pieces = exchange(weighted, "day")
    tiles = points // days // K
    shape = jax.ShapeDtypeStruct((days, tiles * C + 1, 1, K), f32)
    pieces = call(own_points_kernel, shape, pieces, weight_row, name="own_points")
    pieces = exchange(pieces, "day")
    shape = jax.ShapeDtypeStruct((C, points), f32)
    composites = call(finish_kernel, shape, pieces, name="finish")
    return (member.T, centers, composites)


def solution(mesh):
    return jax.shard_map(
        functools.partial(
            on_device, grids=mesh.shape["grid"], days=mesh.shape["day"]
        ),
        mesh=mesh,
        in_specs=(P("day", "grid"), P("grid", None), P()),
        out_specs=(P("day", None), P(), P(None, "grid")),
        check_vma=False,
    )
```

time: 152 us -> 147 us (0.967)
  blocking collectives: 89 us -> 136 us
  starting transfers between devices: 27.2 us -> 0 us
  waiting for transfers between devices: 18.8 us -> 0 us
  Pallas kernels: 15.2 us -> 10.5 us
    all_to_all x6 -> x8, blocking collectives: 89 us -> 136 us  [exchange(): return lax.all_to_all(value, axis, 0, 0)]
    all_to_all x2 -> x0, starting transfers between devices: 25.2 us -> none  [exchange(): return lax.all_to_all(value, axis, 0, 0)]
    all_to_all x2 -> x0, waiting for transfers between devices: 17.5 us -> none  [exchange(): return lax.all_to_all(value, axis, 0, 0)]
    pallas_call x2 -> x1, Pallas kernels: 5.21 us -> 0.86 us  [on_device(): pl.pallas_call(seeds_kernel, in_specs=[smem, pl.BlockSpec(memory_space=pl...]
    ppermute x1 -> x0, starting transfers between devices: 2.01 us -> none  [on_device(): other = lax.ppermute(flipped, 'c', [(0, 1), (1, 0)])]
    pallas_call x6 -> x7, Pallas kernels: 5.78 us -> 5.75 us  [call(): pl.pallas_call(kernel, out_shape=out_shape, name=name, compiler_params=pl...]
  transfers between devices with their start and end apart: 3 -> 0, of which waited for: 3 -> 0; matrix products, arithmetic and copies ran while one was open for 0% -> 0% of each run, Pallas kernels for 0% -> 0%
where the time goes in v3:
time: 147 us
  blocking collectives  136 us (93%)
  Pallas kernels  10.5 us (7%)
    all_to_all x8, blocking collectives, exchange(): return lax.all_to_all(value, axis, 0, 0)  136 us
    pallas_call x7, Pallas kernels, call(): pl.pallas_call(kernel, out_shape=out_shape, name=name, compiler_params=pl...  5.75 us
    pallas_call x1, Pallas kernels, project(): pl.pallas_call(project_kernel, in_specs=[pl.BlockSpec(memory_space=pltpu....  3.88 us

profile of v3, /device:TPU:1, one launch (start us, length us, event | category | flops | bytes accessed | tf_op | source)
XLA Modules:
  0.0 146.7 jit_solution(13701090157626401147)
XLA Ops:
  0.6 0.0 copy-start.1
  0.6 3.9 %project.1 = f32[64,6,1,128]{3,2,1,0:T(1,128)} custom-call(bf16[384,4096]{1,0:T(8,128)(2,1)} %fields_ref.3, bf16[4096,128]{1,0:T(8,128)(2,1)} %basis_ref.1), custom_call_target="tpu_custom_call" | custom-call | tf_op jit(solution)/shard_map/project/pallas_call | solution.py:106
  4.5 0.0 copy-start
  4.5 26.3 %all_to_all.40.pieces_ref = f32[64,6,1,128]{3,2,1,0:T(1,128)S(1)} all-to-all(f32[64,6,1,128]{3,2,1,0:T(1,128)} %project.1), channel_id=1, replica_groups=mesh['grid'=64,'day'=16] {'grid'}, dimensions={0} | all-to-all | bytes 393216 | tf_op jit(solution)/shard_map/all_to_all | solution.py:213
  30.9 0.2 own_rows.1
  31.0 15.8 %all_to_all.41.pieces_ref = f32[64,6,1,128]{3,2,1,0:T(1,128)S(1)} all-to-all(f32[64,6,1,128]{3,2,1,0:T(1,128)S(1)} %own_rows.1), channel_id=1, replica_groups=mesh['grid'=64,'day'=16] {'grid'}, dimensions={0} | all-to-all | bytes 393216 | tf_op jit(solution)/shard_map/all_to_all | solution.py:213
  46.8 0.0 copy-done.1
  46.8 0.9 seeds.1
  47.7 29.4 %all_to_all.42.seeds_ref = f32[16,16,128]{2,1,0:T(8,128)S(1)} all-to-all(f32[16,16,128]{2,1,0:T(8,128)S(1)} %get-tuple-element.9), channel_id=1, replica_groups=mesh['grid'=64,'day'=16] {'day'}, dimensions={0} | all-to-all | bytes 262144 | tf_op jit(solution)/shard_map/all_to_all | solution.py:213
  77.1 1.0 first.1
  78.2 11.7 %all_to_all.43.terms_ref = f32[16,17,1,128]{3,2,1,0:T(1,128)S(1)} all-to-all(f32[16,17,1,128]{3,2,1,0:T(1,128)S(1)} %first.1), channel_id=1, replica_groups=mesh['grid'=64,'day'=16] {'day'}, dimensions={0} | all-to-all | bytes 278528 | tf_op jit(solution)/shard_map/all_to_all | solution.py:213
  89.9 1.1 sweep.2
  91.0 11.7 %all_to_all.44.terms_ref = f32[16,17,1,128]{3,2,1,0:T(1,128)S(1)} all-to-all(f32[16,17,1,128]{3,2,1,0:T(1,128)S(1)} %sweep.2), channel_id=1, replica_groups=mesh['grid'=64,'day'=16] {'day'}, dimensions={0} | all-to-all | bytes 278528 | tf_op jit(solution)/shard_map/all_to_all | solution.py:213
  102.7 1.1 sweep.3
  103.8 11.7 %all_to_all.45.terms_ref = f32[16,17,1,128]{3,2,1,0:T(1,128)S(1)} all-to-all(f32[16,17,1,128]{3,2,1,0:T(1,128)S(1)} %sweep.3), channel_id=1, replica_groups=mesh['grid'=64,'day'=16] {'day'}, dimensions={0} | all-to-all | bytes 278528 | tf_op jit(solution)/shard_map/all_to_all | solution.py:213
  115.6 0.0 copy-done
  115.6 1.4 weigh.1
  116.9 14.2 %all_to_all.46.pieces_ref = f32[16,16,256]{2,1,0:T(8,128)S(1)} all-to-all(f32[16,16,256]{2,1,0:T(8,128)S(1)} %get-tuple-element.13), channel_id=1, replica_groups=mesh['grid'=64,'day'=16] {'day'}, dimensions={0} | all-to-all | bytes 524288 | tf_op jit(solution)/shard_map/all_to_all | solution.py:213
  131.2 0.2 own_points.1
  131.3 14.5 %all_to_all.47.pieces_ref = f32[16,33,1,128]{3,2,1,0:T(1,128)S(1)} all-to-all(f32[16,33,1,128]{3,2,1,0:T(1,128)S(1)} %own_points.1), channel_id=1, replica_groups=mesh['grid'=64,'day'=16] {'day'}, dimensions={0} | all-to-all | bytes 540672 | tf_op jit(solution)/shard_map/all_to_all | solution.py:213
  145.9 0.9 finish.1
Async XLA Ops:
  0.6 46.2 %copy-start.1 = (s32[16]{0:T(128)S(1)}, s32[16]{0:T(128)}, u32[]{:S(2)}) copy-start(s32[16]{0:T(128)} %days_ref.1) | copy-start | bytes 196
  4.5 111.0 %copy-start = (bf16[384,4096]{1,0:T(8,128)(2,1)S(1)}, bf16[384,4096]{1,0:T(8,128)(2,1)}, u32[]{:S(2)}) copy-start(bf16[384,4096]{1,0:T(8,128)(2,1)} %fields_ref.3) | copy-start | bytes 9437188

commit v4 on v3

--- a/solution.py
+++ b/solution.py
@@ -12,6 +12,7 @@
 C = 16
 BLOCKS = 3
 PARTS = 4
+GROUP = 8
 HIGHEST = lax.Precision.HIGHEST
 
 
@@ -60,6 +61,60 @@
 def centers_from(terms_ref):
     total = total_of(terms_ref)
     return total[:C, 0] / column_of(total[C])
+
+
+def early_kernel(
+    days_ref, fields_ref, basis_ref, out_ref, groups_ref, chunk_ref, sem_ref, basis_sem_ref
+):
+    rows = fields_ref.shape[0]
+    first = lax.axis_index("day") * rows
+    basis_load = pltpu.make_async_copy(basis_ref, chunk_ref, basis_sem_ref)
+    basis_load.start()
+    lane = lax.broadcasted_iota(jnp.int32, (1, C * GROUP), 1)
+    loads, picks = [], []
+    for c in range(C):
+        row = days_ref[c] - first
+        inside = jnp.logical_and(row >= 0, row < rows)
+        near = jnp.clip(row, 0, rows - 1)
+        within = lax.rem(near, GROUP)
+        start = pl.multiple_of(near - within, GROUP)
+        loads.append(
+            pltpu.make_async_copy(
+                fields_ref.at[pl.ds(start, GROUP)],
+                groups_ref.at[pl.ds(c * GROUP, GROUP)],
+                sem_ref.at[c],
+            )
+        )
+        loads[-1].start()
+        wanted = jnp.where(inside, c * GROUP + within, -1)
+        picks.append((lane == wanted).astype(jnp.float32))
+    selector = jnp.concatenate(picks, axis=0).astype(jnp.bfloat16)
+    for load in loads:
+        load.wait()
+    chosen = jnp.dot(selector, groups_ref[...], preferred_element_type=jnp.float32)
+    basis_load.wait()
+    seeds = jnp.dot(
+        chosen.astype(jnp.bfloat16), chunk_ref[...], preferred_element_type=jnp.float32
+    )
+    out_ref[...] = jnp.broadcast_to(seeds[None], out_ref.shape)
+
+
+def early_seeds(seed_days, fields, basis, days):
+    points = fields.shape[1]
+    hbm = pl.BlockSpec(memory_space=pltpu.HBM)
+    return pl.pallas_call(
+        early_kernel,
+        in_specs=[pl.BlockSpec(memory_space=pltpu.SMEM), hbm, hbm],
+        out_shape=jax.ShapeDtypeStruct((days, C, K), jnp.float32),
+        scratch_shapes=[
+            pltpu.VMEM((C * GROUP, points), jnp.bfloat16),
+            pltpu.VMEM((points, K), jnp.bfloat16),
+            pltpu.SemaphoreType.DMA((C,)),
+            pltpu.SemaphoreType.DMA,
+        ],
+        name="early_seeds",
+        compiler_params=pltpu.CompilerParams(vmem_limit_bytes=63 << 20),
+    )(seed_days, fields, basis)
 
 
 def project_kernel(
@@ -85,7 +140,6 @@
         load.start()
     for load in basis_loads:
         load.wait()
-    grids = out_ref.shape[0]
     for i in range(blocks):
         loads[i].wait()
         total = None
@@ -96,17 +150,15 @@
                 preferred_element_type=jnp.float32,
             )
             total = part if total is None else total + part
-        each = rows // grids
-        for r in range(each):
-            out_ref[:, i * each + r, 0, :] = total[r * grids : (r + 1) * grids]
-
-
-def project(fields, basis, grids):
+        out_ref[i * rows : (i + 1) * rows, :] = total
+
+
+def project(fields, basis):
     rows, points = fields.shape
     return pl.pallas_call(
         project_kernel,
         in_specs=[pl.BlockSpec(memory_space=pltpu.HBM)] * 2,
-        out_shape=jax.ShapeDtypeStruct((grids, rows // grids, 1, K), jnp.float32),
+        out_shape=jax.ShapeDtypeStruct((rows, K), jnp.float32),
         scratch_shapes=[
             pltpu.VMEM((BLOCKS, rows // BLOCKS, points), jnp.bfloat16),
             pltpu.VMEM((PARTS, points // PARTS, K), jnp.bfloat16),
@@ -114,29 +166,30 @@
             pltpu.SemaphoreType.DMA((PARTS,)),
         ],
         name="project",
+        cost_estimate=pl.CostEstimate(
+            flops=2 * rows * points * K,
+            bytes_accessed=2 * points * (rows + K) + 4 * rows * K,
+            transcendentals=0,
+        ),
         compiler_params=pltpu.CompilerParams(vmem_limit_bytes=63 << 20),
     )(fields, basis)
+
+
+def pack_kernel(partial_ref, seeds_ref, out_ref):
+    grids, own = out_ref.shape[0], out_ref.shape[1] - 1
+    for r in range(own):
+        out_ref[:, r, 0, :] = partial_ref[r * grids : (r + 1) * grids, :]
+    seeds = total_of(seeds_ref)
+    shares = grids // C
+    lane = lax.broadcasted_iota(jnp.int32, (C, K), 1)
+    for q in range(shares):
+        mine = jnp.logical_and(lane >= q * K // shares, lane < (q + 1) * K // shares)
+        out_ref[pl.ds(q, C, stride=shares), own, 0, :] = jnp.where(mine, seeds, 0.0)
 
 
 def own_rows_kernel(pieces_ref, out_ref):
     total = total_of(pieces_ref)
     out_ref[...] = jnp.broadcast_to(total[None], out_ref.shape)
-
-
-def seeds_kernel(days_ref, pieces_ref, flipped_ref, seeds_ref):
-    own = pieces_ref.shape[1]
-    amplitudes = jnp.concatenate([pieces_ref[:, r, 0, :] for r in range(own)], axis=0)
-    rows = amplitudes.shape[0]
-    first = lax.axis_index("day") * rows
-    position = first + lax.broadcasted_iota(jnp.int32, (1, rows), 1)
-    selector = jnp.concatenate(
-        [(position == days_ref[c]).astype(jnp.float32) for c in range(C)], axis=0
-    )
-    seeds = jnp.dot(
-        selector, amplitudes, precision=HIGHEST, preferred_element_type=jnp.float32
-    )
-    flipped_ref[...] = amplitudes.T
-    seeds_ref[...] = jnp.broadcast_to(seeds[None], seeds_ref.shape)
 
 
 def store_terms(flipped, centers, out_ref):
@@ -155,8 +208,16 @@
         out_ref[i, C, :, :] = weight_row
 
 
-def first_kernel(seeds_ref, flipped_ref, out_ref):
-    store_terms(flipped_ref[...], total_of(seeds_ref), out_ref)
+def first_kernel(pieces_ref, flipped_ref, out_ref):
+    grids, own = pieces_ref.shape[0], pieces_ref.shape[1] - 1
+    amplitudes = jnp.concatenate([pieces_ref[:, r, 0, :] for r in range(own)], axis=0)
+    flipped = amplitudes.T
+    flipped_ref[...] = flipped
+    shares = grids // C
+    centers = pieces_ref[pl.ds(0, C, stride=shares), own, 0, :]
+    for q in range(1, shares):
+        centers = centers + pieces_ref[pl.ds(q, C, stride=shares), own, 0, :]
+    store_terms(flipped, centers, out_ref)
 
 
 def sweep_kernel(terms_ref, flipped_ref, out_ref):
@@ -212,24 +273,19 @@
     def exchange(value, axis):
         return lax.all_to_all(value, axis, 0, 0)
 
-    pieces = exchange(project(fields, eof_basis, grids), "grid")
-    shape = jax.ShapeDtypeStruct((grids, own, 1, K), f32)
+    seeds = exchange(early_seeds(seed_days, fields, eof_basis, days), "day")
+    partial_value = project(fields, eof_basis)
+    shape = jax.ShapeDtypeStruct((grids, own + 1, 1, K), f32)
+    pieces = exchange(call(pack_kernel, shape, partial_value, seeds, name="pack"), "grid")
     pieces = exchange(call(own_rows_kernel, shape, pieces, name="own_rows"), "grid")
-
-    smem = pl.BlockSpec(memory_space=pltpu.SMEM)
-    flipped, seeds = pl.pallas_call(
-        seeds_kernel,
-        in_specs=[smem, pl.BlockSpec(memory_space=pltpu.VMEM)],
-        out_shape=[
-            jax.ShapeDtypeStruct((K, rows), f32),
-            jax.ShapeDtypeStruct((days, C, K), f32),
-        ],
-        name="seeds",
-        compiler_params=pltpu.CompilerParams(vmem_limit_bytes=8 << 20),
-    )(seed_days, pieces)
-    seeds = exchange(seeds, "day")
     shape = jax.ShapeDtypeStruct((days, C + 1, 1, K), f32)
-    terms = exchange(call(first_kernel, shape, seeds, flipped, name="first"), "day")
+    flipped, terms = call(
+        first_kernel,
+        [jax.ShapeDtypeStruct((K, rows), f32), shape],
+        pieces,
+        name="first",
+    )
+    terms = exchange(terms, "day")
     for sweep in range(1, ITERS):
         terms = call(sweep_kernel, shape, terms, flipped, name="sweep")
         terms = exchange(terms, "day")

time: 147 us -> 149 us (1.014)
  blocking collectives: 136 us -> 110 us
  starting transfers between devices: 0 us -> 17.9 us
  waiting for transfers between devices: 0 us -> 5.03 us
  Pallas kernels: 10.5 us -> 13.8 us
    all_to_all x8 -> x7, blocking collectives: 136 us -> 110 us  [exchange(): return lax.all_to_all(value, axis, 0, 0)]
    all_to_all x0 -> x1, starting transfers between devices: none -> 17.9 us  [exchange(): return lax.all_to_all(value, axis, 0, 0)]
    all_to_all x0 -> x1, waiting for transfers between devices: none -> 5.03 us  [exchange(): return lax.all_to_all(value, axis, 0, 0)]
    pallas_call x1, Pallas kernels: 0.86 us -> 4.09 us  [early_seeds(): pl.pallas_call(early_kernel, in_specs=[pl.BlockSpec(memory_space=pltpu.SM...]
    pallas_call x7 -> x8, Pallas kernels: 5.75 us -> 5.9 us  [call(): pl.pallas_call(kernel, out_shape=out_shape, name=name, compiler_params=pl...]
  transfers between devices with their start and end apart: 0 -> 1, of which waited for: 0 -> 1; matrix products, arithmetic and copies ran while one was open for 0% -> 0% of each run, Pallas kernels for 0% -> 3%
where the time goes in v4:
time: 149 us; the launch traced here: 148 us
  blocking collectives  110 us (74%)
  starting transfers between devices  17.9 us (12%)
  Pallas kernels  13.8 us (9%)
  waiting for transfers between devices  5.03 us (3%)
    all_to_all x7, blocking collectives, exchange(): return lax.all_to_all(value, axis, 0, 0)  110 us
    all_to_all x1, starting transfers between devices, exchange(): return lax.all_to_all(value, axis, 0, 0)  17.9 us
    pallas_call x8, Pallas kernels, call(): pl.pallas_call(kernel, out_shape=out_shape, name=name, compiler_params=pl...  5.9 us
    all_to_all x1, waiting for transfers between devices, exchange(): return lax.all_to_all(value, axis, 0, 0)  5.03 us
    pallas_call x1, Pallas kernels, early_seeds(): pl.pallas_call(early_kernel, in_specs=[pl.BlockSpec(memory_space=pltpu.SM...  4.09 us
    pallas_call x1, Pallas kernels, project(): pl.pallas_call(project_kernel, in_specs=[pl.BlockSpec(memory_space=pltpu....  3.83 us
  transfers between devices with their start and end apart: 1, of which 1 were waited for; matrix products, arithmetic and copies ran while one was open for 0% of the time, Pallas kernels for 3%

profile of v4, /device:TPU:1, one launch (start us, length us, event | category | flops | bytes accessed | tf_op | source)
XLA Modules:
  0.0 148.3 jit_solution(17221524608768794778)
XLA Ops:
  0.6 4.1 %early_seeds.1 = f32[16,16,128]{2,1,0:T(8,128)} custom-call(s32[16]{0:T(128)} %days_ref.1, bf16[384,4096]{1,0:T(8,128)(2,1)} %fields_ref.5, bf16[4096,128]{1,0:T(8,128)(2,1)} %basis_ref.3), custom_call_target="tpu_custom_call" | custom-call | tf_op jit(solution)/shard_map/early_seeds/pallas_call | solution.py:105
  4.7 17.9 %all-to-all-start = ((f32[16,16,128]{2,1,0:T(8,128)}), f32[16,16,128]{2,1,0:T(8,128)S(1)}, u32[]{:S(2)}, u32[]{:S(2)}) async-start(f32[16,16,128]{2,1,0:T(8,128)} %early_seeds.1), calls=%async_computation | async-start | bytes 262144 | tf_op jit(solution)/shard_map/all_to_all | solution.py:274
  22.6 3.8 %project.1.partial_ref = f32[384,128]{1,0:T(8,128)} custom-call(bf16[384,4096]{1,0:T(8,128)(2,1)} %fields_ref.5, bf16[4096,128]{1,0:T(8,128)(2,1)} %basis_ref.3), custom_call_target="tpu_custom_call" | custom-call | flops 402653184 | bytes 4390912 | tf_op jit(solution)/shard_map/project/pallas_call | solution.py:158
  26.5 0.0 copy-start
  26.5 5.0 %all-to-all-done.seeds_ref = f32[16,16,128]{2,1,0:T(8,128)S(1)} async-done(((f32[16,16,128]{2,1,0:T(8,128)}), f32[16,16,128]{2,1,0:T(8,128)S(1)}, u32[]{:S(2)}, u32[]{:S(2)}) %all-to-all-start) | async-done | bytes 131104 | tf_op jit(solution)/shard_map/all_to_all | solution.py:274
  31.5 0.0 copy-start.1
  31.5 0.9 copy-done.1
  32.4 0.1 pack.1
  32.6 26.2 %all_to_all.40.pieces_ref = f32[64,7,1,128]{3,2,1,0:T(1,128)S(1)} all-to-all(f32[64,7,1,128]{3,2,1,0:T(1,128)S(1)} %pack.1), channel_id=1, replica_groups=mesh['grid'=64,'day'=16] {'grid'}, dimensions={0} | all-to-all | bytes 458752 | tf_op jit(solution)/shard_map/all_to_all | solution.py:274
  58.8 0.2 own_rows.1
  59.0 16.9 %all_to_all.41.pieces_ref = f32[64,7,1,128]{3,2,1,0:T(1,128)S(1)} all-to-all(f32[64,7,1,128]{3,2,1,0:T(1,128)S(1)} %own_rows.1), channel_id=1, replica_groups=mesh['grid'=64,'day'=16] {'grid'}, dimensions={0} | all-to-all | bytes 458752 | tf_op jit(solution)/shard_map/all_to_all | solution.py:274
  75.8 1.1 first.1
  76.9 14.9 %all_to_all.42.terms_ref = f32[16,17,1,128]{3,2,1,0:T(1,128)S(1)} all-to-all(f32[16,17,1,128]{3,2,1,0:T(1,128)S(1)} %get-tuple-element.9), channel_id=1, replica_groups=mesh['grid'=64,'day'=16] {'day'}, dimensions={0} | all-to-all | bytes 278528 | tf_op jit(solution)/shard_map/all_to_all | solution.py:274
  91.8 1.1 sweep.2
  92.9 11.5 %all_to_all.43.terms_ref = f32[16,17,1,128]{3,2,1,0:T(1,128)S(1)} all-to-all(f32[16,17,1,128]{3,2,1,0:T(1,128)S(1)} %sweep.2), channel_id=1, replica_groups=mesh['grid'=64,'day'=16] {'day'}, dimensions={0} | all-to-all | bytes 278528 | tf_op jit(solution)/shard_map/all_to_all | solution.py:274
  104.3 1.1 sweep.3
  105.4 11.7 %all_to_all.44.terms_ref = f32[16,17,1,128]{3,2,1,0:T(1,128)S(1)} all-to-all(f32[16,17,1,128]{3,2,1,0:T(1,128)S(1)} %sweep.3), channel_id=1, replica_groups=mesh['grid'=64,'day'=16] {'day'}, dimensions={0} | all-to-all | bytes 278528 | tf_op jit(solution)/shard_map/all_to_all | solution.py:274
  117.2 0.0 copy-done
  117.2 1.3 weigh.1
  118.5 14.2 %all_to_all.45.pieces_ref = f32[16,16,256]{2,1,0:T(8,128)S(1)} all-to-all(f32[16,16,256]{2,1,0:T(8,128)S(1)} %get-tuple-element.13), channel_id=1, replica_groups=mesh['grid'=64,'day'=16] {'day'}, dimensions={0} | all-to-all | bytes 524288 | tf_op jit(solution)/shard_map/all_to_all | solution.py:274
  132.8 0.2 own_points.1
  132.9 14.5 %all_to_all.46.pieces_ref = f32[16,33,1,128]{3,2,1,0:T(1,128)S(1)} all-to-all(f32[16,33,1,128]{3,2,1,0:T(1,128)S(1)} %own_points.1), channel_id=1, replica_groups=mesh['grid'=64,'day'=16] {'day'}, dimensions={0} | all-to-all | bytes 540672 | tf_op jit(solution)/shard_map/all_to_all | solution.py:274
  147.5 0.9 finish.1
Async XLA Ops:
  4.7 26.8 %all-to-all-start = ((f32[16,16,128]{2,1,0:T(8,128)}), f32[16,16,128]{2,1,0:T(8,128)S(1)}, u32[]{:S(2)}, u32[]{:S(2)}) async-start(f32[16,16,128]{2,1,0:T(8,128)} %early_seeds.1), calls=%async_computation | async-start | bytes 262144 | tf_op jit(solution)/shard_map/all_to_all | solution.py:274
  26.5 90.7 %copy-start = (bf16[384,4096]{1,0:T(8,128)(2,1)S(1)}, bf16[384,4096]{1,0:T(8,128)(2,1)}, u32[]{:S(2)}) copy-start(bf16[384,4096]{1,0:T(8,128)(2,1)} %fields_ref.5) | copy-start | bytes 9437188
  31.5 0.9 copy-start.1

commit v5 on v3

--- a/solution.py
+++ b/solution.py
@@ -103,18 +103,28 @@
 
 def project(fields, basis, grids):
     rows, points = fields.shape
+    fields = pltpu.with_memory_space_constraint(fields, pltpu.HBM)
+    basis = pltpu.with_memory_space_constraint(basis, pltpu.HBM)
     return pl.pallas_call(
         project_kernel,
         in_specs=[pl.BlockSpec(memory_space=pltpu.HBM)] * 2,
-        out_shape=jax.ShapeDtypeStruct((grids, rows // grids, 1, K), jnp.float32),
+        out_specs=[pl.BlockSpec(memory_space=pltpu.VMEM)] * 2,
+        out_shape=[
+            jax.ShapeDtypeStruct((grids, rows // grids, 1, K), jnp.float32),
+            jax.ShapeDtypeStruct((BLOCKS, rows // BLOCKS, points), jnp.bfloat16),
+        ],
         scratch_shapes=[
-            pltpu.VMEM((BLOCKS, rows // BLOCKS, points), jnp.bfloat16),
             pltpu.VMEM((PARTS, points // PARTS, K), jnp.bfloat16),
             pltpu.SemaphoreType.DMA((BLOCKS,)),
             pltpu.SemaphoreType.DMA((PARTS,)),
         ],
         name="project",
-        compiler_params=pltpu.CompilerParams(vmem_limit_bytes=63 << 20),
+        cost_estimate=pl.CostEstimate(
+            flops=2 * rows * points * K,
+            bytes_accessed=2 * points * (rows + K) + 4 * rows * K,
+            transcendentals=0,
+        ),
+        compiler_params=pltpu.CompilerParams(vmem_limit_bytes=16 << 20),
     )(fields, basis)
 
 
@@ -129,9 +139,11 @@
     rows = amplitudes.shape[0]
     first = lax.axis_index("day") * rows
     position = first + lax.broadcasted_iota(jnp.int32, (1, rows), 1)
-    selector = jnp.concatenate(
-        [(position == days_ref[c]).astype(jnp.float32) for c in range(C)], axis=0
-    )
+    lane = lax.broadcasted_iota(jnp.int32, (C, C), 1)
+    sub = lax.broadcasted_iota(jnp.int32, (C, C), 0)
+    days = jnp.where(lane == sub, days_ref[...].astype(jnp.float32), 0.0)
+    wanted = jnp.sum(days, axis=1, keepdims=True)
+    selector = (position.astype(jnp.float32) == wanted).astype(jnp.float32)
     seeds = jnp.dot(
         selector, amplitudes, precision=HIGHEST, preferred_element_type=jnp.float32
     )
@@ -212,21 +224,21 @@
     def exchange(value, axis):
         return lax.all_to_all(value, axis, 0, 0)
 
-    pieces = exchange(project(fields, eof_basis, grids), "grid")
+    pieces, held = project(fields, eof_basis, grids)
+    pieces = exchange(pieces, "grid")
     shape = jax.ShapeDtypeStruct((grids, own, 1, K), f32)
     pieces = exchange(call(own_rows_kernel, shape, pieces, name="own_rows"), "grid")
 
-    smem = pl.BlockSpec(memory_space=pltpu.SMEM)
-    flipped, seeds = pl.pallas_call(
+    flipped, seeds = call(
         seeds_kernel,
-        in_specs=[smem, pl.BlockSpec(memory_space=pltpu.VMEM)],
-        out_shape=[
+        [
             jax.ShapeDtypeStruct((K, rows), f32),
             jax.ShapeDtypeStruct((days, C, K), f32),
         ],
+        seed_days[None, :],
+        pieces,
         name="seeds",
-        compiler_params=pltpu.CompilerParams(vmem_limit_bytes=8 << 20),
-    )(seed_days, pieces)
+    )
     seeds = exchange(seeds, "day")
     shape = jax.ShapeDtypeStruct((days, C + 1, 1, K), f32)
     terms = exchange(call(first_kernel, shape, seeds, flipped, name="first"), "day")
@@ -241,7 +253,7 @@
         jax.ShapeDtypeStruct((days, C, points // days), f32),
     ]
     member, centers, weight_row, weighted = call(
-        weigh_kernel, shapes, terms, flipped, fields, name="weigh"
+        weigh_kernel, shapes, terms, flipped, held.reshape(rows, points), name="weigh"
     )
     pieces = exchange(weighted, "day")
     tiles = points // days // K

time: 147 us -> 145 us (0.986)
    pallas_call x7 -> x8, Pallas kernels: 5.75 us -> 6.08 us  [call(): pl.pallas_call(kernel, out_shape=out_shape, name=name, compiler_params=pl...]
where the time goes in v5:
time: 145 us
  blocking collectives  135 us (93%)
  Pallas kernels  9.29 us (6%)
    all_to_all x8, blocking collectives, exchange(): return lax.all_to_all(value, axis, 0, 0)  135 us
    pallas_call x8, Pallas kernels, call(): pl.pallas_call(kernel, out_shape=out_shape, name=name, compiler_params=pl...  6.08 us
    pallas_call x1, Pallas kernels, project(): pl.pallas_call(project_kernel, in_specs=[pl.BlockSpec(memory_space=pltpu....  3.21 us

profile of v5, /device:TPU:1, one launch (start us, length us, event | category | flops | bytes accessed | tf_op | source)
XLA Modules:
  0.0 145.0 jit_solution(498441577440450693)
XLA Ops:
  0.6 0.0 copy-start
  0.6 3.2 %project.1 = (f32[64,6,1,128]{3,2,1,0:T(1,128)S(1)}, bf16[3,128,4096]{2,1,0:T(8,128)(2,1)S(1)}) custom-call(bf16[384,4096]{1,0:T(8,128)(2,1)} %fields_ref.1, bf16[4096,128]{1,0:T(8,128)(2,1)} %basis_ref.1), custom_call_target="tpu_custom_call" | custom-call | flops 402653184 | bytes 4390912 | tf_op jit(solution)/shard_map/project/pallas_call | solution.py:108
  3.9 25.9 %all_to_all.40.pieces_ref = f32[64,6,1,128]{3,2,1,0:T(1,128)S(1)} all-to-all(f32[64,6,1,128]{3,2,1,0:T(1,128)S(1)} %get-tuple-element.11), channel_id=1, replica_groups=mesh['grid'=64,'day'=16] {'grid'}, dimensions={0} | all-to-all | bytes 393216 | tf_op jit(solution)/shard_map/all_to_all | solution.py:225
  29.7 0.2 own_rows.1
  29.9 15.8 %all_to_all.41.pieces_ref = f32[64,6,1,128]{3,2,1,0:T(1,128)S(1)} all-to-all(f32[64,6,1,128]{3,2,1,0:T(1,128)S(1)} %own_rows.1), channel_id=1, replica_groups=mesh['grid'=64,'day'=16] {'grid'}, dimensions={0} | all-to-all | bytes 393216 | tf_op jit(solution)/shard_map/all_to_all | solution.py:225
  45.7 0.0 copy-done
  45.7 0.3 seeds.1
  46.0 29.4 %all_to_all.42.seeds_ref = f32[16,16,128]{2,1,0:T(8,128)S(1)} all-to-all(f32[16,16,128]{2,1,0:T(8,128)S(1)} %get-tuple-element.12), channel_id=1, replica_groups=mesh['grid'=64,'day'=16] {'day'}, dimensions={0} | all-to-all | bytes 262144 | tf_op jit(solution)/shard_map/all_to_all | solution.py:225
  75.4 1.0 first.1
  76.5 11.7 %all_to_all.43.terms_ref = f32[16,17,1,128]{3,2,1,0:T(1,128)S(1)} all-to-all(f32[16,17,1,128]{3,2,1,0:T(1,128)S(1)} %first.1), channel_id=1, replica_groups=mesh['grid'=64,'day'=16] {'day'}, dimensions={0} | all-to-all | bytes 278528 | tf_op jit(solution)/shard_map/all_to_all | solution.py:225
  88.2 1.1 sweep.2
  89.3 11.7 %all_to_all.44.terms_ref = f32[16,17,1,128]{3,2,1,0:T(1,128)S(1)} all-to-all(f32[16,17,1,128]{3,2,1,0:T(1,128)S(1)} %sweep.2), channel_id=1, replica_groups=mesh['grid'=64,'day'=16] {'day'}, dimensions={0} | all-to-all | bytes 278528 | tf_op jit(solution)/shard_map/all_to_all | solution.py:225
  101.0 1.1 sweep.3
  102.1 11.7 %all_to_all.45.terms_ref = f32[16,17,1,128]{3,2,1,0:T(1,128)S(1)} all-to-all(f32[16,17,1,128]{3,2,1,0:T(1,128)S(1)} %sweep.3), channel_id=1, replica_groups=mesh['grid'=64,'day'=16] {'day'}, dimensions={0} | all-to-all | bytes 278528 | tf_op jit(solution)/shard_map/all_to_all | solution.py:225
  113.9 1.4 weigh.1
  115.2 14.2 %all_to_all.46.pieces_ref = f32[16,16,256]{2,1,0:T(8,128)S(1)} all-to-all(f32[16,16,256]{2,1,0:T(8,128)S(1)} %get-tuple-element.17), channel_id=1, replica_groups=mesh['grid'=64,'day'=16] {'day'}, dimensions={0} | all-to-all | bytes 524288 | tf_op jit(solution)/shard_map/all_to_all | solution.py:225
  129.5 0.2 own_points.1
  129.6 14.5 %all_to_all.47.pieces_ref = f32[16,33,1,128]{3,2,1,0:T(1,128)S(1)} all-to-all(f32[16,33,1,128]{3,2,1,0:T(1,128)S(1)} %own_points.1), channel_id=1, replica_groups=mesh['grid'=64,'day'=16] {'day'}, dimensions={0} | all-to-all | bytes 540672 | tf_op jit(solution)/shard_map/all_to_all | solution.py:225
  144.2 0.9 finish.1
Async XLA Ops:
  0.6 45.1 %copy-start = (s32[16]{0:T(128)S(1)}, s32[16]{0:T(128)}, u32[]{:S(2)}) copy-start(s32[16]{0:T(128)} %param.5) | copy-start | bytes 196

commit v6 on v5

--- a/solution.py
+++ b/solution.py
@@ -162,9 +162,8 @@
         preferred_element_type=jnp.float32,
     )
     weight_row = row_of(jnp.sum(squared, axis=1, keepdims=True))
-    for i in range(out_ref.shape[0]):
-        out_ref[i, :C, 0, :] = numerator
-        out_ref[i, C, :, :] = weight_row
+    out_ref[:C, :] = numerator
+    out_ref[C : C + 1, :] = weight_row
 
 
 def first_kernel(seeds_ref, flipped_ref, out_ref):
@@ -240,11 +239,15 @@
         name="seeds",
     )
     seeds = exchange(seeds, "day")
-    shape = jax.ShapeDtypeStruct((days, C + 1, 1, K), f32)
-    terms = exchange(call(first_kernel, shape, seeds, flipped, name="first"), "day")
+    shape = jax.ShapeDtypeStruct((C + 1, K), f32)
+
+    def spread(terms):
+        copies = jnp.broadcast_to(terms[None, :, None, :], (days, C + 1, 1, K))
+        return exchange(copies, "day")
+
+    terms = spread(call(first_kernel, shape, seeds, flipped, name="first"))
     for sweep in range(1, ITERS):
-        terms = call(sweep_kernel, shape, terms, flipped, name="sweep")
-        terms = exchange(terms, "day")
+        terms = spread(call(sweep_kernel, shape, terms, flipped, name="sweep"))
 
     shapes = [
         jax.ShapeDtypeStruct((C, rows), f32),

time: 145 us -> 145 us (level)
  no operation moved by 1% of the time
where the time goes in v6:
time: 145 us
  blocking collectives  135 us (93%)
  Pallas kernels  8.84 us (6%)
    all_to_all x8, blocking collectives, exchange(): return lax.all_to_all(value, axis, 0, 0)  135 us
    pallas_call x8, Pallas kernels, call(): pl.pallas_call(kernel, out_shape=out_shape, name=name, compiler_params=pl...  5.63 us
    pallas_call x1, Pallas kernels, project(): pl.pallas_call(project_kernel, in_specs=[pl.BlockSpec(memory_space=pltpu....  3.21 us

profile of v6, /device:TPU:1, one launch (start us, length us, event | category | flops | bytes accessed | tf_op | source)
XLA Modules:
  0.0 145.1 jit_solution(4109331376269384096)
XLA Ops:
  0.6 0.0 copy-start
  0.6 3.2 %project.1 = (f32[64,6,1,128]{3,2,1,0:T(1,128)S(1)}, bf16[3,128,4096]{2,1,0:T(8,128)(2,1)S(1)}) custom-call(bf16[384,4096]{1,0:T(8,128)(2,1)} %fields_ref.1, bf16[4096,128]{1,0:T(8,128)(2,1)} %basis_ref.1), custom_call_target="tpu_custom_call" | custom-call | flops 402653184 | bytes 4390912 | tf_op jit(solution)/shard_map/project/pallas_call | solution.py:108
  3.9 25.9 %all_to_all.40.pieces_ref = f32[64,6,1,128]{3,2,1,0:T(1,128)S(1)} all-to-all(f32[64,6,1,128]{3,2,1,0:T(1,128)S(1)} %get-tuple-element.11), channel_id=1, replica_groups=mesh['grid'=64,'day'=16] {'grid'}, dimensions={0} | all-to-all | bytes 393216 | tf_op jit(solution)/shard_map/all_to_all | solution.py:224
  29.7 0.2 own_rows.1
  29.9 15.8 %all_to_all.41.pieces_ref = f32[64,6,1,128]{3,2,1,0:T(1,128)S(1)} all-to-all(f32[64,6,1,128]{3,2,1,0:T(1,128)S(1)} %own_rows.1), channel_id=1, replica_groups=mesh['grid'=64,'day'=16] {'grid'}, dimensions={0} | all-to-all | bytes 393216 | tf_op jit(solution)/shard_map/all_to_all | solution.py:224
  45.7 0.0 copy-done
  45.7 0.3 seeds.1
  46.0 29.4 %all_to_all.42.seeds_ref = f32[16,16,128]{2,1,0:T(8,128)S(1)} all-to-all(f32[16,16,128]{2,1,0:T(8,128)S(1)} %get-tuple-element.12), channel_id=1, replica_groups=mesh['grid'=64,'day'=16] {'day'}, dimensions={0} | all-to-all | bytes 262144 | tf_op jit(solution)/shard_map/all_to_all | solution.py:224
  75.4 0.9 first.1
  76.3 0.2 broadcast_in_dim.9
  76.5 11.7 %all_to_all.43.terms_ref = f32[16,17,1,128]{3,2,1,0:T(1,128)S(1)} all-to-all(f32[16,17,1,128]{3,2,1,0:T(1,128)S(1)} %broadcast_in_dim.9), channel_id=1, replica_groups=mesh['grid'=64,'day'=16] {'day'}, dimensions={0} | all-to-all | bytes 278528 | tf_op jit(solution)/shard_map/all_to_all | solution.py:224
  88.2 0.9 sweep.2
  89.2 0.2 broadcast_in_dim.10
  89.3 11.7 %all_to_all.44.terms_ref = f32[16,17,1,128]{3,2,1,0:T(1,128)S(1)} all-to-all(f32[16,17,1,128]{3,2,1,0:T(1,128)S(1)} %broadcast_in_dim.10), channel_id=1, replica_groups=mesh['grid'=64,'day'=16] {'day'}, dimensions={0} | all-to-all | bytes 278528 | tf_op jit(solution)/shard_map/all_to_all | solution.py:224
  101.1 0.9 sweep.3
  102.0 0.2 broadcast_in_dim.11
  102.2 11.7 %all_to_all.45.terms_ref = f32[16,17,1,128]{3,2,1,0:T(1,128)S(1)} all-to-all(f32[16,17,1,128]{3,2,1,0:T(1,128)S(1)} %broadcast_in_dim.11), channel_id=1, replica_groups=mesh['grid'=64,'day'=16] {'day'}, dimensions={0} | all-to-all | bytes 278528 | tf_op jit(solution)/shard_map/all_to_all | solution.py:224
  113.9 1.4 weigh.1
  115.3 14.2 %all_to_all.46.pieces_ref = f32[16,16,256]{2,1,0:T(8,128)S(1)} all-to-all(f32[16,16,256]{2,1,0:T(8,128)S(1)} %get-tuple-element.17), channel_id=1, replica_groups=mesh['grid'=64,'day'=16] {'day'}, dimensions={0} | all-to-all | bytes 524288 | tf_op jit(solution)/shard_map/all_to_all | solution.py:224
  129.5 0.2 own_points.1
  129.7 14.5 %all_to_all.47.pieces_ref = f32[16,33,1,128]{3,2,1,0:T(1,128)S(1)} all-to-all(f32[16,33,1,128]{3,2,1,0:T(1,128)S(1)} %own_points.1), channel_id=1, replica_groups=mesh['grid'=64,'day'=16] {'day'}, dimensions={0} | all-to-all | bytes 540672 | tf_op jit(solution)/shard_map/all_to_all | solution.py:224
  144.2 0.9 finish.1
Async XLA Ops:
  0.6 45.1 %copy-start = (s32[16]{0:T(128)S(1)}, s32[16]{0:T(128)}, u32[]{:S(2)}) copy-start(s32[16]{0:T(128)} %param.5) | copy-start | bytes 196
